TPU v7x, 128 devices: a whole 4x4x4 slice. The times are simulated.
128 devices in a mesh: row: 4 (over y), col: 32 (over z, x, core).
Axes of the slice: x: 4, y: 4, z: 4, core: 2. Of those that a mesh axis runs over, the one named last changes fastest.
Arguments:
- tokens: bfloat16 [768, 8192], P('col', 'row'), may hold values from -6 to 6
- gate_weight: bfloat16 [8192, 28672], P('row', 'col'), may hold values from -0.0625 to 0.0625
- up_weight: bfloat16 [8192, 28672], P('row', 'col'), may hold values from -0.0625 to 0.0625
- down_weight: bfloat16 [28672, 8192], P('col', 'row'), may hold values from -0.03125 to 0.03125
- mask_gate: int32 [128, 448], P('row', 'col'), may hold values from 0 to 1, as said below
- mask_up: int32 [128, 448], P('row', 'col'), may hold values from 0 to 1, as said below
- mask_down: int32 [448, 128], P('col', 'row'), may hold values from 0 to 1, as said below
- cotangent: bfloat16 [768, 8192], P('col', 'row'), may hold values from -1.5 to 1.5
Outputs:
- output: bfloat16 [768, 8192], P('col', 'row')
- grad_input: bfloat16 [768, 8192], P('col', 'row')
- grad_gate: bfloat16 [8192, 28672], P('row', 'col')
- grad_up: bfloat16 [8192, 28672], P('row', 'col')
- grad_down: bfloat16 [28672, 8192], P('col', 'row')
Inputs may be any that keep to these rules, and one draw needn't show every extreme that they name: `mask_gate`: 1 where a 64 x 64 block of the weight is kept, 0 where it is pruned. `mask_up`: 1 where a 64 x 64 block of the weight is kept, 0 where it is pruned. `mask_down`: 1 where a 64 x 64 block of the weight is kept, 0 where it is pruned.
All inputs are finite; a program needn't handle non-finite values.
Results may differ from a plain program's by a relative error of at most 0.006.
Values may be sent and summed in bfloat16 or wider, within the bound.
No kernel may reach another device: no remote copies, remote signals or barrier semaphores. Data moves between devices by JAX's collectives and lax.ppermute only.
A program may use at most 128 MiB of HBM per device.

v0:
```python
import jax
import jax.numpy as jnp
from jax import lax
from jax.sharding import PartitionSpec as P

BLOCK = 64


def expand(mask):
    return jnp.repeat(jnp.repeat(mask, BLOCK, 0), BLOCK, 1).astype(jnp.bfloat16)


def contract_last(left, right):
    return lax.dot_general(
        left, right, (((1,), (1,)), ((), ())), preferred_element_type=jnp.float32
    )


def contract_first(left, right):
    return lax.dot_general(
        left, right, (((0,), (0,)), ((), ())), preferred_element_type=jnp.float32
    )


def backward_gates(dhid, gate, up):
    sigma = jax.nn.sigmoid(gate)
    dgate = (dhid * up * sigma * (1.0 + gate * (1.0 - sigma))).astype(jnp.bfloat16)
    dup = (dhid * gate * sigma).astype(jnp.bfloat16)
    return (dgate, dup)


def body(tokens, gate_weight, up_weight, down_weight, mask_gate, mask_up, mask_down, cotangent):
    keep_gate = expand(mask_gate)
    keep_up = expand(mask_up)
    keep_down = expand(mask_down)
    w_gate = gate_weight * keep_gate
    w_up = up_weight * keep_up
    w_down = down_weight * keep_down
    width = w_gate.shape[1]
    panel = lax.all_gather(tokens, "col", axis=0, tiled=True)
    stacked = jnp.concatenate([w_gate, w_up], axis=1)
    partial_both = jnp.dot(panel, stacked, preferred_element_type=jnp.float32)
    summed = lax.psum(partial_both, "row")
    gate = summed[:, :width]
    up = summed[:, width:]
    hidden = (jax.nn.silu(gate) * up).astype(jnp.bfloat16)
    output = lax.psum_scatter(
        jnp.dot(hidden, w_down, preferred_element_type=jnp.float32),
        "col",
        scatter_dimension=0,
        tiled=True,
    ).astype(jnp.bfloat16)
    cot_panel = lax.all_gather(cotangent, "col", axis=0, tiled=True)
    partial_dhid = contract_last(cot_panel, w_down)
    dhid = lax.psum(partial_dhid, "row")
    dgate, dup = backward_gates(dhid, gate, up)
    grad_down = (contract_first(hidden, cot_panel) * keep_down).astype(jnp.bfloat16)
    grad_gate = (contract_first(panel, dgate) * keep_gate).astype(jnp.bfloat16)
    grad_up = (contract_first(panel, dup) * keep_up).astype(jnp.bfloat16)
    grad_input = lax.psum_scatter(
        contract_last(dgate, w_gate) + contract_last(dup, w_up),
        "col",
        scatter_dimension=0,
        tiled=True,
    ).astype(jnp.bfloat16)
    return (output, grad_input, grad_gate, grad_up, grad_down)


def solution(mesh):
    return jax.shard_map(
        body,
        mesh=mesh,
        in_specs=(
            P("col", "row"),
            P("row", "col"),
            P("row", "col"),
            P("col", "row"),
            P("row", "col"),
            P("row", "col"),
            P("col", "row"),
            P("col", "row"),
        ),
        out_specs=(
            P("col", "row"),
            P("col", "row"),
            P("row", "col"),
            P("row", "col"),
            P("col", "row"),
        ),
        check_vma=False,
    )
```

profile of v0, /device:TPU:0, one launch (start us, length us, event | category | flops | bytes accessed | tf_op | source)
XLA Modules:
  0.0 472.1 jit_solution(7040883705480512886)
XLA Ops:
  7.2 0.7 all-gather.5.cloned.1.call-update
  7.9 0.7 all-gather.3.cloned.1.call-update
  8.7 0.7 convert_element_type.66
  9.5 0.1 convert_element_type.67
  9.7 0.7 convert_element_type.69
  10.7 6.1 %copy.24 = bf16[2048,896]{0,1:T(8,128)(2,1)} copy(bf16[2048,896]{1,0:T(8,128)(2,1)} %param.9) | data formatting | bytes 7340032 | tf_op args[1]
  16.7 6.1 %copy.25 = bf16[2048,896]{0,1:T(8,128)(2,1)} copy(bf16[2048,896]{1,0:T(8,128)(2,1)} %param.10) | data formatting | bytes 7340032 | tf_op args[2]
  23.2 6.1 %copy.27 = bf16[896,2048]{0,1:T(8,128)(2,1)} copy(bf16[896,2048]{1,0:T(8,128)(2,1)} %param.11) | data formatting | bytes 7340032 | tf_op args[3]
  29.2 4.4 bitcast_multiply_fusion.4
  33.7 1.2 copy-done.1
  34.8 3.6 bitcast_multiply_fusion.2
  38.4 19.5 %all-gather.5.cloned.1.call-done = bf16[768,2048]{1,0:T(8,128)(2,1)} async-done(((bf16[24,2048]{1,0:T(8,128)(2,1)}), bf16[768,2048]{1,0:T(8,128)(2,1)}) %all-gather.5.cloned.1.call-update) | async-done | bytes 3145744 | tf_op jit(solution)/shard_map/all_gather | solution.py:53
  57.9 7.6 %convolution_bitcast_fusion = f32[768,896]{0,1:T(8,128)} fusion(bf16[896,2048]{0,1:T(8,128)(2,1)} %bitcast_multiply_fusion.4, bf16[768,2048]{1,0:T(8,128)(2,1)} %all-gather.5.cloned.1.call-done), kind=kOutput, calls=%fused_computation.18 | convolution fusion | flops 2818572288 | bytes 9568256 | tf_op jit(solution)/shard_map/dot_general | solution.py:14
  65.5 39.1 %all-gather.3.cloned.1.call-done = bf16[768,2048]{1,0:T(8,128)(2,1)} async-done(((bf16[24,2048]{1,0:T(8,128)(2,1)}), bf16[768,2048]{1,0:T(8,128)(2,1)}) %all-gather.3.cloned.1.call-update) | async-done | bytes 3145744 | tf_op jit(solution)/shard_map/all_gather | solution.py:40
  104.7 12.3 %fusion.6 = f32[768,1792]{0,1:T(8,128)} fusion(bf16[768,2048]{1,0:T(8,128)(2,1)} %all-gather.3.cloned.1.call-done, bf16[2048,896]{0,1:T(8,128)(2,1)} %get-tuple-element.25, bf16[2048,896]{0,1:T(8,128)(2,1)} %get-tuple-element.26), kind=kOutput, calls=%fused_computation.11 | convolution fusion | flops 5651824640 | bytes 15990784 | tf_op jit(solution)/shard_map/dot_general | solution.py:42
  117.0 0.2 reduce-scatter.5.cloned.1.call-start
  117.3 157.7 %all-reduce.3.cloned.1.call-done = (f32[768,1792]{0,1:T(8,128)}, f32[768,896]{0,1:T(8,128)}) async-done(((f32[768,1792]{0,1:T(8,128)}, f32[768,896]{0,1:T(8,128)}), (f32[768,1792]{0,1:T(8,128)}, f32[768,896]{0,1:T(8,128)})) %all-reduce.3.cloned.1.call-update) | async-done | bytes 8257552 | tf_op jit(solution)/shard_map/psum | solution.py:43
  274.9 4.3 multiply_convert_fusion.1
  279.4 3.5 fusion.11
  283.0 5.4 %convolution_add_fusion = f32[768,2048]{1,0:T(8,128)} fusion(f32[768,2048]{1,0:T(8,128)S(1)} %fusion.11, bf16[768,896]{0,1:T(8,128)(2,1)S(1)} %get-tuple-element.22, bf16[2048,896]{0,1:T(8,128)(2,1)S(1)} %copy-done.2), kind=kOutput, calls=%fused_computation.12 | convolution fusion | flops 2820145152 | bytes 17629184 | tf_op jit(solution)/shard_map/dot_general | solution.py:14
  288.4 7.4 %fusion.10 = f32[768,2048]{1,0:T(8,128)} fusion(bf16[768,896]{0,1:T(8,128)(2,1)S(1)} %get-tuple-element.24, bf16[896,2048]{0,1:T(8,128)(2,1)} %bitcast_multiply_fusion.4), kind=kOutput, calls=%fused_computation.20 | convolution fusion | flops 2818572288 | bytes 11337728 | tf_op jit(solution)/shard_map/dot_general | solution.py:48
  295.9 2.1 broadcast_in_dim.23
  298.0 6.2 %copy.28 = bf16[896,2048]{1,0:T(8,128)(2,1)} copy(bf16[896,2048]{0,1:T(8,128)(2,1)} %bitcast.41) | data formatting | bytes 7340032 | tf_op jit(solution)/shard_map/convert_element_type | solution.py:10
  304.2 7.3 %fusion.5 = bf16[2048,896]{0,1:T(8,128)(2,1)} fusion(bf16[768,896]{0,1:T(8,128)(2,1)} %copy-done.4, bf16[768,2048]{1,0:T(8,128)(2,1)} %all-gather.3.cloned.1.call-done, bf16[2048,14]{0,1:T(8,128)(2,1)S(1)} %convert_element_type.67), kind=kOutput, calls=%fused_computation.7 | convolution fusion | flops 2824077312 | bytes 8249344 | tf_op jit(solution)/shard_map/dot_general | solution.py:20
  311.5 6.2 %copy.29 = bf16[2048,896]{1,0:T(8,128)(2,1)} copy(bf16[2048,896]{0,1:T(8,128)(2,1)} %fusion.5) | data formatting | bytes 7340032
  317.7 6.9 %fusion.4 = bf16[2048,896]{0,1:T(8,128)(2,1)} fusion(bf16[768,896]{0,1:T(8,128)(2,1)S(1)} %get-tuple-element.22, bf16[768,2048]{1,0:T(8,128)(2,1)} %all-gather.3.cloned.1.call-done, bf16[2048,14]{0,1:T(8,128)(2,1)S(1)} %convert_element_type.70), kind=kOutput, calls=%fused_computation.5 | convolution fusion | flops 2824077312 | bytes 8249344 | tf_op jit(solution)/shard_map/dot_general | solution.py:20
  324.6 6.1 %copy.30 = bf16[2048,896]{1,0:T(8,128)(2,1)} copy(bf16[2048,896]{0,1:T(8,128)(2,1)} %fusion.4) | data formatting | bytes 7340032
  330.6 6.9 %multiply_convert_fusion = bf16[896,2048]{1,0:T(8,128)(2,1)} fusion(bf16[896,2048]{1,0:T(8,128)(2,1)} %copy.28, bf16[768,896]{0,1:T(8,128)(2,1)S(1)} %get-tuple-element.24, bf16[768,2048]{1,0:T(8,128)(2,1)} %all-gather.5.cloned.1.call-done), kind=kOutput, calls=%fused_computation.8 | convolution fusion | flops 2824077312 | bytes 11862016 | tf_op jit(solution)/shard_map/dot_general | solution.py:20
  337.5 37.2 %reduce-scatter.5.cloned.1.call-done = f32[24,2048]{1,0:T(8,128)} async-done(((f32[768,2048]{1,0:T(8,128)}), f32[24,2048]{1,0:T(8,128)}) %reduce-scatter.5.cloned.1.call-update) | async-done | bytes 196624 | tf_op jit(solution)/shard_map/reduce_scatter | solution.py:60
  374.8 1.6 convert_element_type.79
  376.3 87.7 %reduce-scatter.3.cloned.1.call-done = f32[24,2048]{1,0:T(8,128)} async-done(((f32[768,2048]{1,0:T(8,128)}), f32[24,2048]{1,0:T(8,128)}) %reduce-scatter.3.cloned.1.call-update) | async-done | bytes 196624 | tf_op jit(solution)/shard_map/reduce_scatter | solution.py:47
  464.0 1.6 convert_element_type.76
  (25 shorter events, 1.1 us)
Async XLA Ops:
  7.2 50.8 %all-gather.5.cloned.1.call-start = ((), (), s32[]{:S(2)}) async-start(), calls=%async_computation.4 | async-start | bytes 3244032 | tf_op jit(solution)/shard_map/all_gather | solution.py:53
  7.9 96.8 %all-gather.3.cloned.1.call-start = ((), (), s32[]{:S(2)}) async-start(), calls=%async_computation.2 | async-start | bytes 3244032 | tf_op jit(solution)/shard_map/all_gather | solution.py:40
  8.6 266.3 %all-reduce.3.cloned.1.call-start = ((), (), s32[]{:S(2)}) async-start(), calls=%async_computation.6 | async-start | bytes 16515072 | tf_op jit(solution)/shard_map/psum | solution.py:43
  16.7 6.1 %copy-start.5 = (s32[14,32]{1,0:T(8,128)S(1)}, s32[14,32]{1,0:T(8,128)}, u32[]{:S(2)}) copy-start(s32[14,32]{1,0:T(8,128)} %param.14) | copy-start | bytes 5380
  29.2 4.4 copy-start
  29.2 5.6 %copy-start.1 = (bf16[2048,896]{0,1:T(8,128)(2,1)S(1)}, bf16[2048,896]{0,1:T(8,128)(2,1)}, u32[]{:S(2)}) copy-start(bf16[2048,896]{0,1:T(8,128)(2,1)} %copy.25) | copy-start | bytes 11010052
  117.0 257.7 %reduce-scatter.5.cloned.1.call-start = ((), (), s32[]{:S(2)}) async-start(), calls=%async_computation.5 | async-start | bytes 6488064 | tf_op jit(solution)/shard_map/reduce_scatter | solution.py:60
  274.9 4.5 copy-start.3
  279.2 3.7 copy-start.4
  279.4 3.5 copy-start.2
  288.4 175.6 %reduce-scatter.3.cloned.1.call-start = ((), (), s32[]{:S(2)}) async-start(), calls=%async_computation.3 | async-start | bytes 6488064 | tf_op jit(solution)/shard_map/reduce_scatter | solution.py:47
Sparse Core Ops, SparseCore 0:
  10.3 47.6 all-gather.4
  60.2 44.4 all-gather.2
  117.2 157.7 all-reduce.2
  288.5 86.2 reduce-scatter.4
  378.3 85.6 reduce-scatter.2
where the time goes:
time: 473 us; the launch traced here: 472 us
  waiting for transfers between devices  343 us (73%)
  matrix products  57.4 us (12%)
  local copies, waits for them, and re-layouts  40.9 us (9%)
  other arithmetic  16.9 us (4%)
  between operations  13.9 us (3%)
    psum x1, waiting for transfers between devices, body(): summed = lax.psum(partial_both, 'row')  158 us
    reduce_scatter x1, waiting for transfers between devices, body(): lax.psum_scatter(jnp.dot(hidden, w_down, preferred_element_type=jnp.float...  87.7 us
    all_gather x1, waiting for transfers between devices, body(): panel = lax.all_gather(tokens, 'col', axis=0, tiled=True)  39.1 us
    reduce_scatter x1, waiting for transfers between devices, body(): lax.psum_scatter(contract_last(dgate, w_gate) + contract_last(dup, w_up),...  37.2 us
    unnamed x17, local copies, waits for them, and re-layouts  31.7 us
    dot_general x3, matrix products, contract_first(): lax.dot_general(left, right, (((0,), (0,)), ((), ())), preferred_element_...  21.1 us
    all_gather x1, waiting for transfers between devices, body(): cot_panel = lax.all_gather(cotangent, 'col', axis=0, tiled=True)  19.5 us
    dot_general x3, matrix products, contract_last(): lax.dot_general(left, right, (((1,), (1,)), ((), ())), preferred_element_...  16.5 us
  transfers between devices with their start and end apart: 5, of which 5 were waited for; matrix products, arithmetic and copies ran while one was open for 18% of the time, Pallas kernels for 0%

commit v1 on v0

--- a/solution.py
+++ b/solution.py
@@ -4,6 +4,11 @@
 from jax.sharding import PartitionSpec as P
 
 BLOCK = 64
+
+
+def direct_tiles_up(message):
+    d_next = jax.lax.all_gather(message, "row").sum(axis=0)
+    return d_next
 
 
 def expand(mask):
@@ -40,7 +45,7 @@
     panel = lax.all_gather(tokens, "col", axis=0, tiled=True)
     stacked = jnp.concatenate([w_gate, w_up], axis=1)
     partial_both = jnp.dot(panel, stacked, preferred_element_type=jnp.float32)
-    summed = lax.psum(partial_both, "row")
+    summed = direct_tiles_up(partial_both)
     gate = summed[:, :width]
     up = summed[:, width:]
     hidden = (jax.nn.silu(gate) * up).astype(jnp.bfloat16)

time: 473 us -> 576 us (1.22)
  waiting for transfers between devices: 343 us -> 395 us
  local copies, waits for them, and re-layouts: 40.9 us -> 67.7 us
  other arithmetic: 16.9 us -> 39.2 us
    all_gather x0 -> x1, waiting for transfers between devices: none -> 191 us  [direct_tiles_up(): d_next = jax.lax.all_gather(message, 'row').sum(axis=0)]
    psum x1, waiting for transfers between devices: 158 us -> 25.6 us  [body(): dhid = lax.psum(partial_dhid, 'row')]
    all_gather x0 -> x1, local copies, waits for them, and re-layouts: none -> 27.2 us  [direct_tiles_up(): d_next = jax.lax.all_gather(message, 'row').sum(axis=0)]
    reduce_sum x0 -> x1, other arithmetic: none -> 19.3 us  [direct_tiles_up(): d_next = jax.lax.all_gather(message, 'row').sum(axis=0)]
    all_gather x1, waiting for transfers between devices: 39.1 us -> 28.4 us  [body(): panel = lax.all_gather(tokens, 'col', axis=0, tiled=True)]
    unnamed x17 -> x13, local copies, waits for them, and re-layouts: 31.7 us -> 31.2 us
  transfers between devices with their start and end apart: 5 -> 6, of which waited for: 5 -> 6; matrix products, arithmetic and copies ran while one was open for 18% -> 26% of each run, Pallas kernels for 0% -> 0%
where the time goes in v1:
time: 576 us; the launch traced here: 574 us
  waiting for transfers between devices  395 us (69%)
  local copies, waits for them, and re-layouts  67.7 us (12%)
  matrix products  57.5 us (10%)
  other arithmetic  39.2 us (7%)
  between operations  14.2 us (2%)
    all_gather x1, waiting for transfers between devices, direct_tiles_up(): d_next = jax.lax.all_gather(message, 'row').sum(axis=0)  191 us
    reduce_scatter x1, waiting for transfers between devices, body(): lax.psum_scatter(jnp.dot(hidden, w_down, preferred_element_type=jnp.float...  88.1 us
    reduce_scatter x1, waiting for transfers between devices, body(): lax.psum_scatter(contract_last(dgate, w_gate) + contract_last(dup, w_up),...  36.8 us
    unnamed x13, local copies, waits for them, and re-layouts  31.2 us
    all_gather x1, waiting for transfers between devices, body(): panel = lax.all_gather(tokens, 'col', axis=0, tiled=True)  28.4 us
    all_gather x1, local copies, waits for them, and re-layouts, direct_tiles_up(): d_next = jax.lax.all_gather(message, 'row').sum(axis=0)  27.2 us
    psum x1, waiting for transfers between devices, body(): dhid = lax.psum(partial_dhid, 'row')  25.6 us
    all_gather x1, waiting for transfers between devices, body(): cot_panel = lax.all_gather(cotangent, 'col', axis=0, tiled=True)  22.9 us
  transfers between devices with their start and end apart: 6, of which 6 were waited for; matrix products, arithmetic and copies ran while one was open for 26% of the time, Pallas kernels for 0%

profile of v1, /device:TPU:0, one launch (start us, length us, event | category | flops | bytes accessed | tf_op | source)
XLA Modules:
  0.0 573.8 jit_solution(14474079112695014374)
XLA Ops:
  7.2 0.7 all-gather.5.cloned.1.call-update
  7.9 0.7 all-gather.7.cloned.1.call-update
  8.7 0.7 convert_element_type.66
  9.7 0.7 convert_element_type.69
  10.7 6.1 %copy.24 = bf16[2048,896]{0,1:T(8,128)(2,1)} copy(bf16[2048,896]{1,0:T(8,128)(2,1)} %param.9) | data formatting | bytes 7340032 | tf_op args[1]
  16.7 6.0 %copy.25 = bf16[2048,896]{0,1:T(8,128)(2,1)} copy(bf16[2048,896]{1,0:T(8,128)(2,1)} %param.10) | data formatting | bytes 7340032 | tf_op args[2]
  22.8 6.8 %bitcast_multiply_fusion.2 = (bf16[2048,896]{0,1:T(8,128)(2,1)}, bf16[2048,896]{0,1:T(8,128)(2,1)}) fusion(bf16[2048,896]{0,1:T(8,128)(2,1)} %copy.25, bf16[2048,14]{0,1:T(8,128)(2,1)S(1)} %convert_element_type.70, bf16[2048,896]{0,1:T(8,128)(2,1)} %copy.24, bf16[2048,14]{0,1:T(8,128)(2,1)S(1)} %convert_element_type.67), kind=kLoop, calls=%fused_computation.9 | loop fusion | flops 3670016 | bytes 14794752 | tf_op jit(solution)/shard_map/mul | solution.py:42
  29.6 28.4 %all-gather.5.cloned.1.call-done = bf16[768,2048]{1,0:T(8,128)(2,1)} async-done(((bf16[24,2048]{1,0:T(8,128)(2,1)}), bf16[768,2048]{1,0:T(8,128)(2,1)}) %all-gather.5.cloned.1.call-update) | async-done | bytes 3145744 | tf_op jit(solution)/shard_map/all_gather | solution.py:45
  57.9 12.4 %fusion.6 = f32[768,1792]{0,1:T(8,128)} fusion(bf16[768,2048]{1,0:T(8,128)(2,1)} %all-gather.5.cloned.1.call-done, bf16[2048,896]{0,1:T(8,128)(2,1)} %get-tuple-element.23, bf16[2048,896]{0,1:T(8,128)(2,1)} %get-tuple-element.24), kind=kOutput, calls=%fused_computation.11 | convolution fusion | flops 5651824640 | bytes 15990784 | tf_op jit(solution)/shard_map/dot_general | solution.py:47
  71.4 6.1 %copy.27 = bf16[896,2048]{0,1:T(8,128)(2,1)} copy(bf16[896,2048]{1,0:T(8,128)(2,1)} %param.11) | data formatting | bytes 7340032 | tf_op args[3]
  77.5 4.2 bitcast_multiply_fusion.4
  81.7 22.9 %all-gather.7.cloned.1.call-done = bf16[768,2048]{1,0:T(8,128)(2,1)} async-done(((bf16[24,2048]{1,0:T(8,128)(2,1)}), bf16[768,2048]{1,0:T(8,128)(2,1)}) %all-gather.7.cloned.1.call-update) | async-done | bytes 3145744 | tf_op jit(solution)/shard_map/all_gather | solution.py:58
  104.7 7.6 %convolution_bitcast_fusion = f32[768,896]{0,1:T(8,128)} fusion(bf16[896,2048]{0,1:T(8,128)(2,1)} %bitcast_multiply_fusion.4, bf16[768,2048]{1,0:T(8,128)(2,1)} %all-gather.7.cloned.1.call-done), kind=kOutput, calls=%fused_computation.18 | convolution fusion | flops 2818572288 | bytes 9568256 | tf_op jit(solution)/shard_map/dot_general | solution.py:19
  112.5 191.3 %all-gather.9.cloned.1.call-done = f32[3072,1792]{0,1:T(8,128)} async-done(((f32[768,1792]{0,1:T(8,128)}), f32[3072,1792]{0,1:T(8,128)}) %all-gather.9.cloned.1.call-update) | async-done | bytes 22020112 | tf_op jit(solution)/shard_map/all_gather | solution.py:10
  303.8 27.2 %reshape.22 = f32[4,768,1792]{1,0,2:T(4,128)} reshape(f32[3072,1792]{0,1:T(8,128)} %all-gather.9.cloned.1.call-done) | data formatting | bytes 44040192 | tf_op jit(solution)/shard_map/all_gather | solution.py:10
  331.0 19.3 %reduce_sum.9 = f32[768,1792]{0,1:T(8,128)} reduce(f32[4,768,1792]{1,0,2:T(4,128)} %reshape.22, f32[]{:T(128)} %constant.2.clone.1), dimensions={0}, to_apply=%region_0.0 | reduce | flops 4128768 | bytes 27525124 | tf_op jit(solution)/shard_map/reduce_sum | solution.py:10
  350.3 25.6 %all-reduce.2.cloned.1.call-done = f32[768,896]{0,1:T(8,128)} async-done(((f32[768,896]{0,1:T(8,128)}), f32[768,896]{0,1:T(8,128)}) %all-reduce.2.cloned.1.call-update) | async-done | bytes 2752528 | tf_op jit(solution)/shard_map/psum | solution.py:60
  375.9 4.3 multiply_convert_fusion.1
  380.3 3.5 fusion.11
  383.9 5.4 convolution_add_fusion
  389.6 7.5 %fusion.10 = f32[768,2048]{1,0:T(8,128)} fusion(bf16[768,896]{0,1:T(8,128)(2,1)S(1)} %get-tuple-element.22, bf16[896,2048]{0,1:T(8,128)(2,1)} %bitcast_multiply_fusion.4), kind=kOutput, calls=%fused_computation.20 | convolution fusion | flops 2818572288 | bytes 11337728 | tf_op jit(solution)/shard_map/dot_general | solution.py:53
  397.1 2.1 broadcast_in_dim.23
  399.2 6.3 %copy.28 = bf16[896,2048]{1,0:T(8,128)(2,1)} copy(bf16[896,2048]{0,1:T(8,128)(2,1)} %bitcast.43) | data formatting | bytes 7340032 | tf_op jit(solution)/shard_map/convert_element_type | solution.py:15
  405.5 7.3 %fusion.5 = bf16[2048,896]{0,1:T(8,128)(2,1)} fusion(bf16[768,896]{0,1:T(8,128)(2,1)} %copy-done.2, bf16[768,2048]{1,0:T(8,128)(2,1)} %all-gather.5.cloned.1.call-done, bf16[2048,14]{0,1:T(8,128)(2,1)S(1)} %convert_element_type.67), kind=kOutput, calls=%fused_computation.7 | convolution fusion | flops 2824077312 | bytes 8249344 | tf_op jit(solution)/shard_map/dot_general | solution.py:25
  412.8 6.2 %copy.29 = bf16[2048,896]{1,0:T(8,128)(2,1)} copy(bf16[2048,896]{0,1:T(8,128)(2,1)} %fusion.5) | data formatting | bytes 7340032
  419.0 6.9 %fusion.4 = bf16[2048,896]{0,1:T(8,128)(2,1)} fusion(bf16[768,896]{0,1:T(8,128)(2,1)S(1)} %get-tuple-element.20, bf16[768,2048]{1,0:T(8,128)(2,1)} %all-gather.5.cloned.1.call-done, bf16[2048,14]{0,1:T(8,128)(2,1)S(1)} %convert_element_type.70), kind=kOutput, calls=%fused_computation.5 | convolution fusion | flops 2824077312 | bytes 8249344 | tf_op jit(solution)/shard_map/dot_general | solution.py:25
  425.9 6.1 %copy.30 = bf16[2048,896]{1,0:T(8,128)(2,1)} copy(bf16[2048,896]{0,1:T(8,128)(2,1)} %fusion.4) | data formatting | bytes 7340032
  432.0 6.9 %multiply_convert_fusion = bf16[896,2048]{1,0:T(8,128)(2,1)} fusion(bf16[896,2048]{1,0:T(8,128)(2,1)} %copy.28, bf16[768,896]{0,1:T(8,128)(2,1)S(1)} %get-tuple-element.22, bf16[768,2048]{1,0:T(8,128)(2,1)} %all-gather.7.cloned.1.call-done), kind=kOutput, calls=%fused_computation.8 | convolution fusion | flops 2824077312 | bytes 11862016 | tf_op jit(solution)/shard_map/dot_general | solution.py:25
  438.9 36.8 %reduce-scatter.5.cloned.1.call-done = f32[24,2048]{1,0:T(8,128)} async-done(((f32[768,2048]{1,0:T(8,128)}), f32[24,2048]{1,0:T(8,128)}) %reduce-scatter.5.cloned.1.call-update) | async-done | bytes 196624 | tf_op jit(solution)/shard_map/reduce_scatter | solution.py:65
  475.7 1.6 convert_element_type.79
  477.3 88.1 %reduce-scatter.3.cloned.1.call-done = f32[24,2048]{1,0:T(8,128)} async-done(((f32[768,2048]{1,0:T(8,128)}), f32[24,2048]{1,0:T(8,128)}) %reduce-scatter.3.cloned.1.call-update) | async-done | bytes 196624 | tf_op jit(solution)/shard_map/reduce_scatter | solution.py:52
  565.4 1.6 convert_element_type.76
  (26 shorter events, 2.4 us)
Async XLA Ops:
  7.2 50.8 %all-gather.5.cloned.1.call-start = ((), (), s32[]{:S(2)}) async-start(), calls=%async_computation.2 | async-start | bytes 3244032 | tf_op jit(solution)/shard_map/all_gather | solution.py:45
  7.9 96.8 %all-gather.7.cloned.1.call-start = ((), (), s32[]{:S(2)}) async-start(), calls=%async_computation.4 | async-start | bytes 3244032 | tf_op jit(solution)/shard_map/all_gather | solution.py:58
  8.6 295.2 %all-gather.9.cloned.1.call-start = ((), (), s32[]{:S(2)}) async-start(), calls=%async_computation.7 | async-start | bytes 27525120 | tf_op jit(solution)/shard_map/all_gather | solution.py:10
  70.4 0.7 copy-start.3
  70.4 305.5 %all-reduce.2.cloned.1.call-start = ((), (), s32[]{:S(2)}) async-start(), calls=%async_computation.5 | async-start | bytes 5505024 | tf_op jit(solution)/shard_map/psum | solution.py:60
  112.3 363.4 %reduce-scatter.5.cloned.1.call-start = ((), (), s32[]{:S(2)}) async-start(), calls=%async_computation.6 | async-start | bytes 6488064 | tf_op jit(solution)/shard_map/reduce_scatter | solution.py:65
  375.9 4.5 copy-start.1
  380.2 3.7 copy-start.2
  380.3 3.5 copy-start
  389.3 176.1 %reduce-scatter.3.cloned.1.call-start = ((), (), s32[]{:S(2)}) async-start(), calls=%async_computation.3 | async-start | bytes 6488064 | tf_op jit(solution)/shard_map/reduce_scatter | solution.py:52
Sparse Core Ops, SparseCore 0:
  10.3 47.6 all-gather.4
  60.2 44.4 all-gather.6
  106.4 197.3 all-gather.8
  306.0 69.7 all-reduce.1
  389.4 86.1 reduce-scatter.4
  479.7 85.6 reduce-scatter.2
